TPU v7x, 32 devices: a whole 2x2x4 slice. The times are simulated.
32 devices in a mesh: dp: 4 (over z), expert: 8 (over y, x, core).
Axes of the slice: x: 2, y: 2, z: 4, core: 2. Of those that a mesh axis runs over, the one named last changes fastest.
Arguments:
- layer_input: bfloat16 [16384, 768], P(('dp', 'expert')), may hold values from -6 to 6
- seq_lengths: int32 [32], P(('dp', 'expert')), may hold values from 64 to 512, as said below
- routes: int32 [16384, 2], P(('dp', 'expert')), may hold values from 0 to 9, all different within a row
- ln1_gain: float32 [768], replicated, may hold values from 0.25 to 1.75
- w_query: bfloat16 [768, 768], replicated, may hold values from -0.21875 to 0.21875
- w_key: bfloat16 [768, 768], replicated, may hold values from -0.21875 to 0.21875
- w_value: bfloat16 [768, 768], replicated, may hold values from -0.21875 to 0.21875
- w_output: bfloat16 [768, 768], replicated, may hold values from -0.625 to 0.625
- ln2_gain: float32 [768], replicated, may hold values from 0.25 to 1.75
- w_router: float32 [768, 10], replicated, may hold values from -0.15625 to 0.15625
- frozen_in: bfloat16 [2, 768, 3072], replicated, may hold values from -0.21875 to 0.21875
- frozen_out: bfloat16 [2, 3072, 768], replicated, may hold values from -0.15625 to 0.15625
- new_in: bfloat16 [8, 768, 3072], P('expert'), may hold values from -0.21875 to 0.21875
- new_out: bfloat16 [8, 3072, 768], P('expert'), may hold values from -0.15625 to 0.15625
- cotangent: bfloat16 [16384, 768], P(('dp', 'expert')), may hold values from -6 to 6
Outputs:
- output: float32 [16384, 768], P(('dp', 'expert'))
- grad_input: float32 [16384, 768], P(('dp', 'expert'))
- grad_ln1: float32 [768], replicated
- grad_w_query: float32 [768, 768], replicated
- grad_w_key: float32 [768, 768], replicated
- grad_w_value: float32 [768, 768], replicated
- grad_w_output: float32 [768, 768], replicated
- grad_ln2: float32 [768], replicated
- grad_router: float32 [768, 10], replicated
- grad_new_in: float32 [8, 768, 3072], P('expert', None, 'dp')
- grad_new_out: float32 [8, 3072, 768], P('expert', 'dp')
Inputs may be any that keep to these rules, and one draw needn't show every extreme that they name: `seq_lengths`: in every draw one sequence has exactly 512 valid tokens and another exactly 64. `routes`: the two experts of a token differ.
All inputs are finite; a program needn't handle non-finite values.
Results may differ from a plain program's by a relative error of at most 0.013.
Values may be sent and summed in bfloat16 or wider, within the bound.
A program may use at most 192 MiB of HBM per device.

v0:
```python
import jax
import jax.numpy as jnp
from jax import lax
from jax.sharding import PartitionSpec as P

HEADS = 12
FROZEN = 2
NORM_EPS = 1e-05
GELU_SCALE = 0.7978845608028654
GELU_CUBIC = 0.044715
MASK_VALUE = -1e30


def normalize(values):
    center = values - jnp.mean(values, -1, keepdims=True)
    factor = lax.rsqrt(jnp.mean(center * center, -1, keepdims=True) + NORM_EPS)
    return (center * factor, factor)


def norm_back(grad_normed, normed, factor):
    return factor * (
        grad_normed
        - jnp.mean(grad_normed, -1, keepdims=True)
        - normed * jnp.mean(grad_normed * normed, -1, keepdims=True)
    )


def gelu_value(values):
    return (
        0.5
        * values
        * (1.0 + jnp.tanh(GELU_SCALE * (values + GELU_CUBIC * values * values * values)))
    )


def gelu_slope(values):
    tangent = jnp.tanh(GELU_SCALE * (values + GELU_CUBIC * values * values * values))
    return 0.5 * (1.0 + tangent) + 0.5 * values * (1.0 - tangent * tangent) * GELU_SCALE * (
        1.0 + 3.0 * GELU_CUBIC * values * values
    )


def route_slots(route_rows, length, capacity, new_count):
    tokens = route_rows.shape[0]
    pair_route = jnp.concatenate([route_rows[:, 0], route_rows[:, 1]])
    position = jnp.arange(tokens, dtype=jnp.int32)
    valid = position < length
    pair_valid = jnp.concatenate([valid, valid])
    expert_new = pair_route - FROZEN
    onehot = (
        (expert_new[:, None] == jnp.arange(new_count, dtype=jnp.int32)[None, :])
        & pair_valid[:, None]
    ).astype(jnp.int32)
    before = jnp.cumsum(onehot, 0, dtype=jnp.int32) - onehot
    rank = jnp.sum(before * onehot, 1, dtype=jnp.int32)
    is_new = jnp.sum(onehot, 1, dtype=jnp.int32) > 0
    kept_new = is_new & (rank < capacity)
    slot = jnp.where(kept_new, expert_new * capacity + rank, -1)
    match = slot[None, :] == jnp.arange(new_count * capacity, dtype=jnp.int32)[:, None]
    filled = jnp.any(match, 1)
    slot_pair = jnp.sum(
        jnp.where(match, jnp.arange(2 * tokens, dtype=jnp.int32)[None, :], 0), 1, dtype=jnp.int32
    )
    return (valid, kept_new, slot, filled, slot_pair)


def on_device(
    layer_input,
    seq_lengths,
    routes,
    ln1_gain,
    w_query,
    w_key,
    w_value,
    w_output,
    ln2_gain,
    w_router,
    frozen_in,
    frozen_out,
    new_in,
    new_out,
    cotangent,
):
    tokens, width = layer_input.shape
    head_dim = width // HEADS
    local_new = new_in.shape[0]
    new_count = local_new * lax.axis_size("expert")
    total_experts = FROZEN + new_count
    capacity = 2 * tokens // total_experts
    f32 = jnp.float32
    bf16 = jnp.bfloat16
    scale_value = head_dim ** (-0.5)
    input_rows = layer_input.astype(f32)
    normed_one_f, factor_one = normalize(input_rows)
    normed_one = (normed_one_f * ln1_gain).astype(bf16)
    query_rows = jnp.dot(normed_one, w_query, preferred_element_type=f32).astype(bf16)
    key_rows = jnp.dot(normed_one, w_key, preferred_element_type=f32).astype(bf16)
    value_rows = jnp.dot(normed_one, w_value, preferred_element_type=f32).astype(bf16)
    head_query = query_rows.reshape(tokens, HEADS, head_dim)
    head_key = key_rows.reshape(tokens, HEADS, head_dim)
    head_value = value_rows.reshape(tokens, HEADS, head_dim)
    position = jnp.arange(tokens, dtype=jnp.int32)
    allowed = (position[None, :] <= position[:, None]) & (position[None, :] < seq_lengths[0])

    def masked_scores():
        raw_scores = (
            jnp.einsum("qhd,khd->hqk", head_query, head_key, preferred_element_type=f32)
            * scale_value
        )
        return jnp.where(allowed[None], raw_scores, MASK_VALUE)

    scores = masked_scores()
    peak_value = jnp.max(scores, -1, keepdims=True)
    expo_values = jnp.exp(scores - peak_value)
    row_total = jnp.sum(expo_values, -1, keepdims=True)
    log_total = peak_value + jnp.log(row_total)
    probs_low = (expo_values / row_total).astype(bf16)
    merged = (
        jnp.einsum("hqk,khd->qhd", probs_low, head_value, preferred_element_type=f32)
        .reshape(tokens, width)
        .astype(bf16)
    )
    hidden = input_rows + jnp.dot(merged, w_output, preferred_element_type=f32)
    normed_two_f, factor_two = normalize(hidden)
    normed_two = normed_two_f * ln2_gain
    expert_input = normed_two.astype(bf16)
    logits = jnp.dot(
        normed_two, w_router, precision=lax.Precision.HIGHEST, preferred_element_type=f32
    )
    logit_peak = jnp.max(logits, -1, keepdims=True)
    logit_expo = jnp.exp(logits - logit_peak)
    prob = logit_expo / jnp.sum(logit_expo, -1, keepdims=True)
    route_hot = (
        routes[:, :, None] == jnp.arange(total_experts, dtype=jnp.int32)[None, None, :]
    ).astype(f32)
    chosen = jnp.sum(route_hot * prob[:, None, :], -1)
    chosen_total = jnp.sum(chosen, 1, keepdims=True)
    gates = chosen / chosen_total
    valid, kept_new, slot, filled, slot_pair = route_slots(
        routes, seq_lengths[0], capacity, new_count
    )
    frozen_hot = route_hot[:, :, :FROZEN] * valid.astype(f32)[:, None, None]
    frozen_weight = jnp.sum(frozen_hot * gates[:, :, None], 1)
    frozen_pre = jnp.einsum("td,fde->fte", expert_input, frozen_in, preferred_element_type=f32)
    frozen_act = gelu_value(frozen_pre).astype(bf16)
    frozen_res = jnp.einsum("fte,fed->ftd", frozen_act, frozen_out, preferred_element_type=f32)
    mixture = jnp.sum(frozen_weight.T[:, :, None] * frozen_res, 0)
    slot_token = slot_pair % tokens
    send_rows = jnp.where(filled[:, None], expert_input[slot_token], jnp.zeros((), bf16)).reshape(
        new_count, capacity, width
    )
    received = lax.all_to_all(send_rows, "expert", split_axis=0, concat_axis=1, tiled=True)
    new_pre = jnp.einsum("erd,edf->erf", received, new_in, preferred_element_type=f32)
    new_act = gelu_value(new_pre).astype(bf16)
    new_res = jnp.einsum("erf,efd->erd", new_act, new_out, preferred_element_type=f32).astype(bf16)
    returned = lax.all_to_all(new_res, "expert", split_axis=1, concat_axis=0, tiled=True)
    safe_slot = jnp.maximum(slot, 0)
    pair_res = jnp.where(
        kept_new[:, None], returned.reshape(new_count * capacity, width)[safe_slot].astype(f32), 0.0
    )
    pair_gate = jnp.concatenate([gates[:, 0], gates[:, 1]])
    kept_gate = jnp.where(kept_new, pair_gate, 0.0)
    mixture = (
        mixture
        + kept_gate[:tokens, None] * pair_res[:tokens]
        + kept_gate[tokens:, None] * pair_res[tokens:]
    )
    output = hidden + mixture
    grad_out = cotangent.astype(f32)
    frozen_dot = jnp.einsum("td,ftd->tf", grad_out, frozen_res)
    new_dot = jnp.sum(grad_out[None] * pair_res.reshape(2, tokens, width), -1).T
    grad_gate = jnp.sum(frozen_hot * frozen_dot[:, None, :], -1) + new_dot
    mixing = jnp.sum(grad_gate * gates, 1, keepdims=True)
    grad_chosen = (grad_gate - mixing) / chosen_total
    grad_prob = jnp.sum(route_hot * grad_chosen[:, :, None], 1)
    grad_logits = prob * (grad_prob - jnp.sum(prob * grad_prob, -1, keepdims=True))
    grad_router = jnp.dot(
        normed_two.T, grad_logits, precision=lax.Precision.HIGHEST, preferred_element_type=f32
    )
    frozen_grad_res = (frozen_weight.T[:, :, None] * grad_out[None]).astype(bf16)
    frozen_grad_act = jnp.einsum(
        "ftd,fed->fte", frozen_grad_res, frozen_out, preferred_element_type=f32
    )
    frozen_grad_pre = (frozen_grad_act * gelu_slope(frozen_pre)).astype(bf16)
    grad_expert_in = jnp.einsum(
        "fte,fde->td", frozen_grad_pre, frozen_in, preferred_element_type=f32
    )
    slot_gate = jnp.where(filled, pair_gate[slot_pair], 0.0)
    grad_send = (
        (slot_gate[:, None] * grad_out[slot_token]).astype(bf16).reshape(new_count, capacity, width)
    )
    grad_received = lax.all_to_all(grad_send, "expert", split_axis=0, concat_axis=1, tiled=True)
    new_grad_act = jnp.einsum("erd,efd->erf", grad_received, new_out, preferred_element_type=f32)
    new_grad_pre = (new_grad_act * gelu_slope(new_pre)).astype(bf16)
    grad_sent_rows = jnp.einsum(
        "erf,edf->erd", new_grad_pre, new_in, preferred_element_type=f32
    ).astype(bf16)
    grad_back = lax.all_to_all(grad_sent_rows, "expert", split_axis=1, concat_axis=0, tiled=True)
    back_pair = jnp.where(
        kept_new[:, None],
        grad_back.reshape(new_count * capacity, width)[safe_slot].astype(f32),
        0.0,
    )
    grad_expert_in = grad_expert_in + back_pair[:tokens] + back_pair[tokens:]
    local_in = jnp.einsum("erd,erf->edf", received, new_grad_pre, preferred_element_type=f32)
    local_out = jnp.einsum("erf,erd->efd", new_act, grad_received, preferred_element_type=f32)
    grad_new_in, grad_new_out = (
        lax.psum_scatter(
            local_in.astype(jnp.bfloat16), "dp", scatter_dimension=2, tiled=True
        ).astype(jnp.float32),
        lax.psum_scatter(
            local_out.astype(jnp.bfloat16), "dp", scatter_dimension=1, tiled=True
        ).astype(jnp.float32),
    )
    grad_normed_two = grad_expert_in + jnp.dot(
        grad_logits, w_router.T, precision=lax.Precision.HIGHEST, preferred_element_type=f32
    )
    grad_ln2 = jnp.sum(grad_normed_two * normed_two_f, 0)
    grad_hidden = grad_out + norm_back(grad_normed_two * ln2_gain, normed_two_f, factor_two)
    grad_attn = grad_hidden.astype(bf16)
    grad_w_output = jnp.dot(merged.T, grad_attn, preferred_element_type=f32)
    grad_merged = jnp.dot(grad_attn, w_output.T, preferred_element_type=f32).astype(bf16)
    grad_heads = grad_merged.reshape(tokens, HEADS, head_dim)
    probs_again = jnp.exp(masked_scores() - log_total)
    grad_probs = jnp.einsum("qhd,khd->hqk", grad_heads, head_value, preferred_element_type=f32)
    grad_scores = (
        probs_again * (grad_probs - jnp.sum(probs_again * grad_probs, -1, keepdims=True))
    ).astype(bf16)
    grad_query_rows = (
        (
            jnp.einsum("hqk,khd->qhd", grad_scores, head_key, preferred_element_type=f32)
            * scale_value
        )
        .astype(bf16)
        .reshape(tokens, width)
    )
    grad_key_rows = (
        (
            jnp.einsum("hqk,qhd->khd", grad_scores, head_query, preferred_element_type=f32)
            * scale_value
        )
        .astype(bf16)
        .reshape(tokens, width)
    )
    grad_value_rows = (
        jnp.einsum("hqk,qhd->khd", probs_again.astype(bf16), grad_heads, preferred_element_type=f32)
        .astype(bf16)
        .reshape(tokens, width)
    )
    grad_w_query = jnp.dot(normed_one.T, grad_query_rows, preferred_element_type=f32)
    grad_w_key = jnp.dot(normed_one.T, grad_key_rows, preferred_element_type=f32)
    grad_w_value = jnp.dot(normed_one.T, grad_value_rows, preferred_element_type=f32)
    grad_normed_one = (
        jnp.dot(grad_query_rows, w_query.T, preferred_element_type=f32)
        + jnp.dot(grad_key_rows, w_key.T, preferred_element_type=f32)
        + jnp.dot(grad_value_rows, w_value.T, preferred_element_type=f32)
    )
    grad_ln1 = jnp.sum(grad_normed_one * normed_one_f, 0)
    grad_input = grad_hidden + norm_back(grad_normed_one * ln1_gain, normed_one_f, factor_one)
    summed = lax.psum(
        (grad_ln1, grad_w_query, grad_w_key, grad_w_value, grad_w_output, grad_ln2, grad_router),
        ("dp", "expert"),
    )
    return (
        output,
        grad_input,
        summed[0],
        summed[1],
        summed[2],
        summed[3],
        summed[4],
        summed[5],
        summed[6],
        grad_new_in,
        grad_new_out,
    )


def solution(mesh):
    placed = (
        P(("dp", "expert"), None),
        P(("dp", "expert")),
        P(("dp", "expert"), None),
        P(),
        P(),
        P(),
        P(),
        P(),
        P(),
        P(),
        P(),
        P(),
        P("expert", None, None),
        P("expert", None, None),
        P(("dp", "expert"), None),
    )
    return jax.shard_map(
        on_device,
        mesh=mesh,
        in_specs=placed,
        out_specs=(
            P(("dp", "expert"), None),
            P(("dp", "expert"), None),
            P(),
            P(),
            P(),
            P(),
            P(),
            P(),
            P(),
            P("expert", None, "dp"),
            P("expert", "dp", None),
        ),
        check_vma=False,
    )
```

profile of v0, /device:TPU:0, one launch (start us, length us, event | category | flops | bytes accessed | tf_op | source)
XLA Modules:
  0.0 569.3 jit_solution(2203841953963201932)
XLA Ops:
  14.4 2.3 reduce-window.6
  17.9 2.4 convolution_convert_fusion.3
  20.6 3.3 convolution_convert_fusion.4
  25.4 2.4 convolution_convert_fusion.5
  27.8 2.3 copy.80
  30.1 3.0 fusion.30
  33.2 3.8 fusion.7
  37.9 3.8 fusion.73
  43.1 1.7 fusion.125
  50.4 4.0 gather_fusion
  57.2 5.2 all-to-all-start
  64.2 5.8 %gather_fusion.2 = f32[816]{0:T(1024)} fusion(f32[1024]{0:T(1024)S(1)} %get-tuple-element.39, s32[1024]{0:T(1024)} %pad_clamp_fusion), kind=kCustom, calls=%fused_computation.2 | custom fusion | bytes 9792 | tf_op jit(solution)/shard_map/gather | solution.py:188
  71.4 4.0 gather_fusion.3
  75.5 2.9 gather.27
  79.1 3.0 multiply_convert_fusion.5
  82.1 4.3 all-to-all-start.2
  86.4 2.8 reshape.485
  89.1 10.5 %fusion.26 = f32[816,3072]{1,0:T(8,128)} fusion(bf16[816,768]{1,0:T(8,128)(2,1)} %reshape.485, bf16[1,768,3072]{2,1,0:T(8,128)(2,1)} %param.27), kind=kOutput, calls=%fused_computation.45 | convolution fusion | flops 3850371072 | bytes 15998976 | tf_op jit(solution)/shard_map/erd,edf->erf/dot_general | solution.py:153
  99.7 4.6 all-to-all-done.2
  104.3 2.3 reshape.489
  106.5 11.4 %fusion.29 = bf16[1,3072,768]{2,1,0:T(8,128)(2,1)} fusion(bf16[816,768]{1,0:T(8,128)(2,1)} %reshape.489, f32[816,3072]{1,0:T(8,128)} %fusion.26), kind=kOutput, calls=%fused_computation.48 | convolution fusion | flops 3875291136 | bytes 15998976 | tf_op jit(solution)/shard_map/erf,erd->efd/dot_general | solution.py:206
  118.0 7.6 %fusion.79 = f32[512,2,3072]{2,0,1:T(8,128)S(1)} fusion(bf16[2,768,3072]{2,1,0:T(8,128)(2,1)} %param.25, bf16[512,768]{1,0:T(8,128)(2,1)S(1)} %multiply_convert_fusion.12), kind=kOutput, calls=%fused_computation.120 | convolution fusion | flops 4831838208 | bytes 22806528 | tf_op jit(solution)/shard_map/td,fde->fte/dot_general | solution.py:144
  125.6 13.5 %fusion.19 = f32[2,512,768]{2,1,0:T(8,128)S(1)} fusion(bf16[2,3072,768]{2,1,0:T(8,128)(2,1)} %param.26, f32[512,2,3072]{2,0,1:T(8,128)S(1)} %fusion.79), kind=kOutput, calls=%fused_computation.36 | convolution fusion | flops 4860149760 | bytes 25165824 | tf_op jit(solution)/shard_map/fte,fed->ftd/dot_general | solution.py:146
  140.8 6.2 %fusion.34 = f32[512,1,2]{2,1,0:T(1,128)} fusion(f32[2,512,768]{2,1,0:T(8,128)S(1)} %fusion.19, bf16[512,768,1]{1,0,2:T(8,128)(2,1)S(1)} %bitcast.168), kind=kOutput, calls=%fused_computation.60 | convolution fusion | flops 1572864 | bytes 3936256 | tf_op jit(solution)/shard_map/td,ftd->tf/dot_general | solution.py:170
  154.0 3.4 multiply_reduce_fusion.1
  157.5 9.9 %fusion.64 = bf16[1,816,768]{2,1,0:T(8,128)(2,1)S(1)} fusion(bf16[1,3072,768]{2,1,0:T(8,128)(2,1)} %param.28, f32[816,3072]{1,0:T(8,128)} %fusion.26), kind=kOutput, calls=%fused_computation.100 | convolution fusion | flops 3873558528 | bytes 15998976 | tf_op jit(solution)/shard_map/erf,efd->erd/dot_general | solution.py:155
  167.4 3.4 copy.116
  171.3 10.3 %reduce.10 = bf16[816,768]{1,0:T(8,128)(2,1)} reduce(bf16[816,1,768]{2,1,0:T(2,128)(2,1)} %bitcast.160, bf16[]{:T(256)} %broadcast.531), dimensions={1}, to_apply=%bitcast.148.reduce_sub_computation | reduce | bytes 2506754
  181.7 2.3 reshape.542
  183.9 4.3 all-to-all-start.1
  188.2 12.6 %fusion.14 = bf16[816,3072]{1,0:T(8,128)(2,1)S(1)} fusion(f32[816,3072]{1,0:T(8,128)} %fusion.26, bf16[816,768]{1,0:T(8,128)(2,1)} %reshape.489, bf16[1,3072,768]{2,1,0:T(8,128)(2,1)} %param.28), kind=kOutput, calls=%fused_computation.31 | convolution fusion | flops 3897999360 | bytes 21012480 | tf_op jit(solution)/shard_map/erd,efd->erf/dot_general | solution.py:193
  200.8 8.2 %fusion.67 = bf16[1,816,768]{2,1,0:T(8,128)(2,1)S(1)} fusion(bf16[816,3072]{1,0:T(8,128)(2,1)S(1)} %fusion.14, bf16[1,768,3072]{2,1,0:T(8,128)(2,1)} %param.27), kind=kOutput, calls=%fused_computation.101 | convolution fusion | flops 3850997760 | bytes 10985472 | tf_op jit(solution)/shard_map/erf,edf->erd/dot_general | solution.py:195
  209.0 3.3 copy.115
  212.4 10.5 %reduce.11 = bf16[816,768]{1,0:T(8,128)(2,1)} reduce(bf16[816,1,768]{2,1,0:T(2,128)(2,1)} %bitcast.161, bf16[]{:T(256)} %broadcast.531), dimensions={1}, to_apply=%bitcast.147.reduce_sub_computation | reduce | bytes 2506754
  222.9 2.3 reshape.544
  225.1 4.3 all-to-all-start.3
  230.2 8.8 %fusion.28 = bf16[1,768,3072]{2,1,0:T(8,128)(2,1)} fusion(bf16[816,768]{1,0:T(8,128)(2,1)} %reshape.485, bf16[816,3072]{1,0:T(8,128)(2,1)} %copy-done.66), kind=kOutput, calls=%fused_computation.47 | convolution fusion | flops 3852730368 | bytes 10985472 | tf_op jit(solution)/shard_map/erd,erf->edf/dot_general | solution.py:205
  239.0 6.5 %reshape.543 = bf16[816,1,768]{2,1,0:T(2,128)(2,1)} reshape(bf16[8,2,39168]{2,1,0:T(2,128)(2,1)} %all-to-all-done.1) | data formatting | bytes 2506752
  245.6 3.1 copy.114
  248.6 6.5 %reshape.545 = bf16[816,1,768]{2,1,0:T(2,128)(2,1)} reshape(bf16[8,2,39168]{2,1,0:T(2,128)(2,1)} %all-to-all-done.3) | data formatting | bytes 2506752
  255.2 2.9 copy.113
  258.1 7.0 %gather_fusion.1 = bf16[1024,768]{1,0:T(8,128)(2,1)} fusion(bf16[816,768]{1,0:T(8,128)(2,1)} %bitcast.154, s32[1024]{0:T(1024)S(1)} %broadcast_clamp_fusion), kind=kCustom, calls=%fused_computation.1 | custom fusion | bytes 3149824 | tf_op jit(solution)/shard_map/gather | solution.py:159
  265.1 7.0 %gather_fusion.4 = bf16[1024,768]{1,0:T(8,128)(2,1)} fusion(bf16[816,768]{1,0:T(8,128)(2,1)} %bitcast.155, s32[1024]{0:T(1024)S(1)} %broadcast_clamp_fusion), kind=kCustom, calls=%fused_computation.4 | custom fusion | bytes 3149824 | tf_op jit(solution)/shard_map/gather | solution.py:201
  272.2 5.9 %fusion.33 = (f32[1024]{0:T(1024)}, f32[1024,768]{1,0:T(8,128)}, f32[1024,768]{1,0:T(8,128)}) fusion(f32[512,768]{1,0:T(8,128)S(1)} %convert_element_type.157, bf16[1024,768]{1,0:T(8,128)(2,1)} %gather_fusion.1, pred[1024]{0:T(1024)(128)(4,1)} %copy-done.61, bf16[1024,768]{1,0:T(8,128)(2,1)} %gather_fusion.4), kind=kLoop, calls=%fused_computation.55 | loop fusion | flops 4717568 | bytes 11015168 | tf_op jit(solution)/shard_map/reduce_sum | solution.py:171
  281.7 3.4 fusion.93
  285.1 21.6 %multiply_reduce_fusion.2 = (f32[768]{0:T(1024)}, f32[512]{0:T(512)}, f32[512]{0:T(512)}, f32[512,768]{1,0:T(8,128)}) fusion(f32[512]{0:T(512)S(1)} %copy-done.41, f32[512,768]{1,0:T(8,128)} %copy-done.2, f32[512]{0:T(512)S(1)} %broadcast_multiply_fusion.4, f32[768]{0:T(1024)S(1)} %copy-done.37, f32[512,768]{1,0:T(8,128)} %fusion.93, ...), kind=kOutput, calls=%fused_computation.89 | convolution fusion | flops 9729341440 | bytes 40912896 | tf_op jit(solution)/shard_map/fte,fde->td/dot_general | solution.py:185
  308.2 4.9 multiply_add_fusion.2
  315.1 8.0 %fusion.70 = bf16[12,64,512]{2,1,0:T(8,128)(2,1)S(1)} fusion(bf16[512,12,64]{0,2,1:T(8,128)(2,1)} %bitcast.166, f32[12,512]{1,0:T(8,128)} %log_add_fusion, f32[12,512,512]{1,2,0:T(8,128)} %copy-done.1, pred[512,512]{0,1:T(8,128)(4,1)} %fusion.78), kind=kOutput, calls=%fused_computation.106 | convolution fusion | flops 415629312 | bytes 14442496 | tf_op jit(solution)/shard_map/hqk,qhd->khd/dot_general | solution.py:246
  324.1 2.4 fusion.112
  326.5 10.2 %multiply_reduce_fusion = (f32[12,512]{1,0:T(8,128)S(1)}, f32[12,512,512]{1,2,0:T(8,128)}) fusion(f32[12,512]{1,0:T(8,128)S(1)} %copy-done.33, f32[12,512,512]{1,2,0:T(8,128)} %copy-done.1, pred[512,512]{0,1:T(8,128)(4,1)S(1)} %copy-done.13, bf16[512,12,64]{0,2,1:T(8,128)(2,1)S(1)} %bitcast.167, bf16[512,12,64]{0,2,1:T(8,128)(2,1)S(1)} %bitcast.165), kind=kOutput, calls=%fused_computation.18 | convolution fusion | flops 418375680 | bytes 27049984 | tf_op jit(solution)/shard_map/qhd,khd->hqk/dot_general | solution.py:225
  336.8 7.3 %multiply_convert_fusion = bf16[12,512,512]{1,2,0:T(8,128)(2,1)S(1)} fusion(f32[12,512,512]{1,2,0:T(8,128)} %get-tuple-element.55, f32[12,512]{1,0:T(8,128)S(1)} %get-tuple-element.54, f32[12,512]{1,0:T(8,128)S(1)} %copy-done.33, f32[12,512,512]{1,2,0:T(8,128)S(1)} %bitcast.153, pred[512,512]{0,1:T(8,128)(4,1)S(1)} %copy-done.13), kind=kLoop, calls=%fused_computation.17 | loop fusion | flops 18874368 | bytes 31768576 | tf_op jit(solution)/shard_map/convert_element_type | solution.py:228
  344.1 2.0 multiply_convert_fusion.8
  347.0 2.4 fusion.114
  351.4 2.4 fusion.116
  353.9 2.2 fusion.83
  357.5 2.7 fusion.74
  360.2 2.3 fusion.127
  363.7 3.1 fusion.53
  366.8 45.1 %all-reduce = (f32[768]{0:T(1024)}, f32[768]{0:T(1024)}, f32[768,10]{0,1:T(8,128)}) all-reduce(f32[768]{0:T(1024)S(1)} %get-tuple-element.13, f32[768]{0:T(1024)} %get-tuple-element.11, f32[768,10]{0,1:T(8,128)} %fusion.74), channel_id=1, replica_groups=mesh['dp'=4,'expert'=8] {'dp','expert'}, use_global_device_ids=true, to_apply=%region_29.30 | all-reduce | flops 9216 | bytes 73728 | tf_op jit(solution)/shard_map/psum | solution.py:260
  413.3 3.1 fusion.52
  416.4 2.8 convert_element_type.180
  419.2 2.8 convert_element_type.177
  422.1 129.5 %all-reduce.4.cloned.1.call-done = (f32[768,768]{1,0:T(8,128)}, f32[768,768]{1,0:T(8,128)}, f32[768,768]{1,0:T(8,128)}, f32[768,768]{1,0:T(8,128)}) async-done(((f32[768,768]{1,0:T(8,128)}, f32[768,768]{1,0:T(8,128)}, f32[768,768]{1,0:T(8,128)}, f32[768,768]{1,0:T(8,128)}), (f32[768,768]{1,0:T(8,128)}, f32[768,768]{1,0:T(8,128)}, f32[768,768]{1,0:T(8,128)}, ...) | async-done | bytes 9437200 | tf_op jit(solution)/shard_map/psum | solution.py:260
  551.6 3.4 copy.122
  (220 shorter events, 53.9 us)
Async XLA Ops:
  8.0 17.4 %copy-start = (bf16[768,768]{1,0:T(8,128)(2,1)S(1)}, bf16[768,768]{1,0:T(8,128)(2,1)}, u32[]{:S(2)}) copy-start(bf16[768,768]{1,0:T(8,128)(2,1)} %param.21) | copy-start | bytes 3538948
  12.1 13.2 %copy-start.47 = (f32[512]{0:T(512)}, f32[512]{0:T(512)S(1)}, u32[]{:S(2)}) copy-start(f32[512]{0:T(512)S(1)} %broadcast_multiply_fusion.5) | copy-start | bytes 6148
  13.6 11.7 %copy-start.52 = (f32[512]{0:T(512)}, f32[512]{0:T(512)S(1)}, u32[]{:S(2)}) copy-start(f32[512]{0:T(512)S(1)} %add_rsqrt_fusion.1) | copy-start | bytes 6148
  14.4 31.7 %copy-start.42 = (s32[512,1]{0,1:T(1,128)}, s32[512,1]{0,1:T(1,128)S(1)}, u32[]{:S(2)}) copy-start(s32[512,1]{0,1:T(1,128)S(1)} %get-tuple-element.42) | copy-start | bytes 6148
  14.4 31.7 %copy-start.43 = (s32[512,1]{0,1:T(1,128)}, s32[512,1]{0,1:T(1,128)S(1)}, u32[]{:S(2)}) copy-start(s32[512,1]{0,1:T(1,128)S(1)} %get-tuple-element.43) | copy-start | bytes 6148
  17.9 2.7 copy-start.6
  20.6 9.5 %copy-start.8 = (bf16[512,768]{0,1:T(8,128)(2,1)}, bf16[512,768]{0,1:T(8,128)(2,1)S(1)}, u32[]{:S(2)}) copy-start(bf16[512,768]{0,1:T(8,128)(2,1)S(1)} %copy.82) | copy-start | bytes 2359300
  25.4 4.7 copy-start.10
  33.1 4.6 copy-start.1
  33.2 4.7 copy-start.32
  33.2 4.7 copy-start.12
  33.2 4.7 copy-start.14
  37.0 4.7 copy-start.35
  37.9 3.8 copy-start.63
  41.7 1.3 copy-start.24
  41.7 1.3 copy-start.34
  42.7 6.2 %copy-start.2 = (f32[512,768]{1,0:T(8,128)}, f32[512,768]{1,0:T(8,128)S(1)}, u32[]{:S(2)}) copy-start(f32[512,768]{1,0:T(8,128)S(1)} %get-tuple-element.50) | copy-start | bytes 4718596
  42.7 3.3 copy-start.38
  42.7 3.4 copy-start.36
  42.7 3.4 copy-start.62
  43.1 5.8 %copy-start.40 = (f32[512]{0:T(512)}, f32[512]{0:T(512)S(1)}, u32[]{:S(2)}) copy-start(f32[512]{0:T(512)S(1)} %add_rsqrt_fusion) | copy-start | bytes 6148
  44.8 3.6 copy-start.31
  46.0 2.3 copy-start.45
  46.1 2.3 copy-start.50
  46.1 2.3 copy-start.44
  49.2 6.7 %copy-start.60 = (pred[8,102]{1,0:T(8,128)(4,1)}, pred[8,102]{1,0:T(8,128)(4,1)S(1)}, u32[]{:S(2)}) copy-start(pred[8,102]{1,0:T(8,128)(4,1)S(1)} %broadcast_in_dim.76) | copy-start | bytes 2452
  57.2 24.9 %all-to-all-start = ((bf16[8,102,768]{2,1,0:T(8,128)(2,1)}), bf16[8,102,768]{2,1,0:T(8,128)(2,1)}, u32[]{:S(2)}, u32[]{:S(2)}) async-start(bf16[8,102,768]{2,1,0:T(8,128)(2,1)} %broadcast_select_fusion), calls=%async_computation | async-start | bytes 2555904 | tf_op jit(solution)/shard_map/all_to_all | solution.py:152
  82.1 22.2 %all-to-all-start.2 = ((bf16[8,102,768]{2,1,0:T(8,128)(2,1)}), bf16[8,102,768]{2,1,0:T(8,128)(2,1)}, u32[]{:S(2)}, u32[]{:S(2)}) async-start(bf16[8,102,768]{2,1,0:T(8,128)(2,1)} %multiply_convert_fusion.5), calls=%async_computation.2 | async-start | bytes 2555904 | tf_op jit(solution)/shard_map/all_to_all | solution.py:192
  86.3 330.0 %reduce-scatter.5.cloned.1.call-start = ((), (), s32[]{:S(2)}) async-start(), calls=%async_computation.7 | async-start | bytes 5898240 | tf_op jit(solution)/shard_map/reduce_scatter | solution.py:211
  125.6 13.5 %copy-start.67 = (f32[512,2,3072]{2,0,1:T(8,128)}, f32[512,2,3072]{2,0,1:T(8,128)S(1)}, u32[]{:S(2)}) copy-start(f32[512,2,3072]{2,0,1:T(8,128)S(1)} %fusion.79) | copy-start | bytes 37748740
  125.6 15.2 %copy-start.17 = (bf16[512,768]{1,0:T(8,128)(2,1)S(1)}, bf16[512,768]{1,0:T(8,128)(2,1)}, u32[]{:S(2)}) copy-start(bf16[512,768]{1,0:T(8,128)(2,1)} %param.29) | copy-start | bytes 2359300
  139.1 1.7 copy-start.18
  140.8 7.9 %copy-start.39 = (s32[512,2]{0,1:T(2,128)S(1)}, s32[512,2]{0,1:T(2,128)}, u32[]{:S(2)}) copy-start(s32[512,2]{0,1:T(2,128)} %param.17) | copy-start | bytes 12292
  150.0 4.0 copy-start.59
  183.9 41.2 %all-to-all-start.1 = ((bf16[8,2,39168]{2,1,0:T(2,128)(2,1)}), bf16[8,2,39168]{2,1,0:T(2,128)(2,1)}, u32[]{:S(2)}, u32[]{:S(2)}) async-start(bf16[8,2,39168]{2,1,0:T(2,128)(2,1)} %reshape.542), calls=%async_computation.1 | async-start | bytes 2506752 | tf_op jit(solution)/shard_map/all_to_all | solution.py:156
  200.8 8.3 %copy-start.66 = (bf16[816,3072]{1,0:T(8,128)(2,1)}, bf16[816,3072]{1,0:T(8,128)(2,1)S(1)}, u32[]{:S(2)}) copy-start(bf16[816,3072]{1,0:T(8,128)(2,1)S(1)} %fusion.14) | copy-start | bytes 15040516
  225.1 23.5 %all-to-all-start.3 = ((bf16[8,2,39168]{2,1,0:T(2,128)(2,1)}), bf16[8,2,39168]{2,1,0:T(2,128)(2,1)}, u32[]{:S(2)}, u32[]{:S(2)}) async-start(bf16[8,2,39168]{2,1,0:T(2,128)(2,1)} %reshape.544), calls=%async_computation.3 | async-start | bytes 2506752 | tf_op jit(solution)/shard_map/all_to_all | solution.py:198
  229.4 189.8 %reduce-scatter.3.cloned.1.call-start = ((), (), s32[]{:S(2)}) async-start(), calls=%async_computation.6 | async-start | bytes 5898240 | tf_op jit(solution)/shard_map/reduce_scatter | solution.py:208
  239.0 312.6 %all-reduce.4.cloned.1.call-start = ((), (), s32[]{:S(2)}) async-start(), calls=%async_computation.8 | async-start | bytes 18874368 | tf_op jit(solution)/shard_map/psum | solution.py:260
  272.2 13.0 %copy-start.41 = (f32[512]{0:T(512)S(1)}, f32[512]{0:T(512)}, u32[]{:S(2)}) copy-start(f32[512]{0:T(512)} %copy-done.40) | copy-start | bytes 6148
  281.7 25.1 %copy-start.51 = (f32[512]{0:T(512)}, f32[512]{0:T(512)S(1)}, u32[]{:S(2)}) copy-start(f32[512]{0:T(512)S(1)} %multiply_reduce_fusion.7) | copy-start | bytes 6148
  308.1 4.9 copy-start.64
  313.1 40.8 %copy-start.4 = (f32[512,768]{1,0:T(8,128)}, f32[512,768]{1,0:T(8,128)S(1)}, u32[]{:S(2)}) copy-start(f32[512,768]{1,0:T(8,128)S(1)} %get-tuple-element.37) | copy-start | bytes 4718596
  315.1 9.0 %copy-start.7 = (bf16[512,768]{1,0:T(8,128)(2,1)S(1)}, bf16[512,768]{1,0:T(8,128)(2,1)}, u32[]{:S(2)}) copy-start(bf16[512,768]{1,0:T(8,128)(2,1)} %param.15) | copy-start | bytes 2359300
  315.1 9.0 %copy-start.48 = (f32[512]{0:T(512)S(1)}, f32[512]{0:T(512)}, u32[]{:S(2)}) copy-start(f32[512]{0:T(512)} %copy-done.47) | copy-start | bytes 6148
  315.1 9.0 %copy-start.53 = (f32[512]{0:T(512)S(1)}, f32[512]{0:T(512)}, u32[]{:S(2)}) copy-start(f32[512]{0:T(512)} %copy-done.52) | copy-start | bytes 6148
  315.1 9.0 %copy-start.56 = (f32[768]{0:T(1024)S(1)}, f32[768]{0:T(1024)}, u32[]{:S(2)}) copy-start(f32[768]{0:T(1024)} %param.18) | copy-start | bytes 9220
  323.1 3.4 copy-start.13
  323.1 3.4 copy-start.15
  323.1 3.4 copy-start.16
  323.1 3.4 copy-start.33
  324.1 12.7 %slice-start = ((s8[12582912]{0:T(1024)(128)(4,1)}), s8[4194304]{0:T(1024)(128)(4,1)S(1)}, s32[]{:S(2)}) async-start(s8[12582912]{0:T(1024)(128)(4,1)} %bitcast.152), calls=%async_computation.9 | async-start | bytes 8388608
  326.5 10.2 %slice-start.1 = ((s8[12582912]{0:T(1024)(128)(4,1)}), s8[4194304]{0:T(1024)(128)(4,1)S(1)}, s32[]{:S(2)}) async-start(s8[12582912]{0:T(1024)(128)(4,1)} %bitcast.152), calls=%async_computation.10 | async-start | bytes 8388608
  326.5 10.2 %slice-start.2 = ((s8[12582912]{0:T(1024)(128)(4,1)}), s8[4194304]{0:T(1024)(128)(4,1)S(1)}, s32[]{:S(2)}) async-start(s8[12582912]{0:T(1024)(128)(4,1)} %bitcast.152), calls=%async_computation.11 | async-start | bytes 8388608
  336.7 7.3 %copy-start.11 = (bf16[512,768]{0,1:T(8,128)(2,1)S(1)}, bf16[512,768]{0,1:T(8,128)(2,1)}, u32[]{:S(2)}) copy-start(bf16[512,768]{0,1:T(8,128)(2,1)} %copy-done.10) | copy-start | bytes 2359300
  346.1 3.3 copy-start.9
  350.6 3.3 copy-start.25
  356.1 1.4 copy-start.3
  357.5 5.1 copy-start.20
  357.5 5.1 copy-start.65
  363.7 49.6 %copy-start.5 = (f32[512,768]{1,0:T(8,128)S(1)}, f32[512,768]{1,0:T(8,128)}, u32[]{:S(2)}) copy-start(f32[512,768]{1,0:T(8,128)} %copy-done.4) | copy-start | bytes 4718596
  551.6 3.4 copy-start.23
  554.9 2.5 copy-start.22
  557.5 2.5 copy-start.21
  (14 other events, 13.1 us)
Sparse Core Ops, SparseCore 0:
  118.1 85.1 reduce-scatter.4
  239.1 87.3 reduce-scatter.2
Sparse Core Ops, SparseCore 1:
  356.2 195.3 all-reduce.3
where the time goes:
time: 579 us; the launch traced here: 569 us
  matrix products  172 us (30%)
  waiting for transfers between devices  134 us (23%)
  local copies, waits for them, and re-layouts  99.2 us (17%)
  other arithmetic  83.1 us (14%)
  blocking collectives  45.1 us (8%)
  starting transfers between devices  18.1 us (3%)
  between operations  17.6 us (3%)
    psum x1, waiting for transfers between devices, on_device(): lax.psum((grad_ln1, grad_w_query, grad_w_key, grad_w_value, grad_w_output...  129 us
    psum x1, blocking collectives, on_device(): lax.psum((grad_ln1, grad_w_query, grad_w_key, grad_w_value, grad_w_output...  45.1 us
    unnamed x153, local copies, waits for them, and re-layouts  43.1 us
    dot_general x1, matrix products, on_device(): jnp.einsum('fte,fde->td', frozen_grad_pre, frozen_in, preferred_element_t...  21.6 us
    unnamed x4, other arithmetic  21.5 us
    dot_general x1, matrix products, on_device(): jnp.einsum('fte,fed->ftd', frozen_act, frozen_out, preferred_element_type...  13.5 us
    dot_general x1, matrix products, on_device(): jnp.einsum('erd,efd->erf', grad_received, new_out, preferred_element_type...  12.6 us
  transfers between devices with their start and end apart: 7, of which 2 were waited for; matrix products, arithmetic and copies ran while one was open for 49% of the time, Pallas kernels for 0%

commit v1 on v0

--- a/solution.py
+++ b/solution.py
@@ -258,8 +258,19 @@
     grad_ln1 = jnp.sum(grad_normed_one * normed_one_f, 0)
     grad_input = grad_hidden + norm_back(grad_normed_one * ln1_gain, normed_one_f, factor_one)
     summed = lax.psum(
-        (grad_ln1, grad_w_query, grad_w_key, grad_w_value, grad_w_output, grad_ln2, grad_router),
-        ("dp", "expert"),
+        lax.psum(
+            (
+                grad_ln1,
+                grad_w_query,
+                grad_w_key,
+                grad_w_value,
+                grad_w_output,
+                grad_ln2,
+                grad_router,
+            ),
+            "expert",
+        ),
+        "dp",
     )
     return (
         output,

time: 579 us -> 878 us (1.52)
  waiting for transfers between devices: 134 us -> 429 us
    psum x0 -> x1, waiting for transfers between devices: none -> 311 us  [on_device(): lax.psum(lax.psum((grad_ln1, grad_w_query, grad_w_key, grad_w_value, grad...]
    psum x0 -> x1, blocking collectives: none -> 21.6 us  [on_device(): lax.psum(lax.psum((grad_ln1, grad_w_query, grad_w_key, grad_w_value, grad...]
    psum x1, blocking collectives: 45.1 us -> 25 us  [on_device(): lax.psum((grad_ln1, grad_w_query, grad_w_key, grad_w_value, grad_w_output...]
    psum x1, waiting for transfers between devices: 129 us -> 117 us  [on_device(): lax.psum((grad_ln1, grad_w_query, grad_w_key, grad_w_value, grad_w_output...]
    unnamed x153 -> x155, local copies, waits for them, and re-layouts: 43.1 us -> 42.3 us
  transfers between devices with their start and end apart: 7 -> 8, of which waited for: 2 -> 3; matrix products, arithmetic and copies ran while one was open for 49% -> 22% of each run, Pallas kernels for 0% -> 0%
where the time goes in v1:
time: 878 us; the launch traced here: 868 us
  waiting for transfers between devices  429 us (49%)
  matrix products  177 us (20%)
  local copies, waits for them, and re-layouts  98 us (11%)
  other arithmetic  81.8 us (9%)
  blocking collectives  46.6 us (5%)
  starting transfers between devices  18.2 us (2%)
  between operations  17.8 us (2%)
    psum x1, waiting for transfers between devices, on_device(): lax.psum(lax.psum((grad_ln1, grad_w_query, grad_w_key, grad_w_value, grad...  311 us
    psum x1, waiting for transfers between devices, on_device(): lax.psum((grad_ln1, grad_w_query, grad_w_key, grad_w_value, grad_w_output...  117 us
    unnamed x155, local copies, waits for them, and re-layouts  42.3 us
    psum x1, blocking collectives, on_device(): lax.psum((grad_ln1, grad_w_query, grad_w_key, grad_w_value, grad_w_output...  25 us
    unnamed x4, other arithmetic  21.9 us
    psum x1, blocking collectives, on_device(): lax.psum(lax.psum((grad_ln1, grad_w_query, grad_w_key, grad_w_value, grad...  21.6 us
    dot_general x1, matrix products, on_device(): jnp.einsum('fte,fde->td', frozen_grad_pre, frozen_in, preferred_element_t...  21.5 us
  transfers between devices with their start and end apart: 8, of which 3 were waited for; matrix products, arithmetic and copies ran while one was open for 22% of the time, Pallas kernels for 0%

profile of v1, /device:TPU:0, one launch (start us, length us, event | category | flops | bytes accessed | tf_op | source)
XLA Modules:
  0.0 868.0 jit_solution(11732499905417853261)
XLA Ops:
  14.4 2.3 reduce-window.6
  17.9 2.4 convolution_convert_fusion.3
  20.6 3.3 convolution_convert_fusion.4
  25.4 2.4 convolution_convert_fusion.5
  27.8 2.3 copy.80
  30.1 3.0 fusion.30
  33.2 3.8 fusion.7
  37.8 3.9 fusion.73
  49.8 4.0 gather_fusion
  53.8 2.3 gather.22
  56.1 2.5 broadcast_select_fusion
  58.6 5.2 all-to-all-start
  63.8 7.6 fusion.79
  71.4 13.5 %fusion.19 = f32[2,512,768]{2,1,0:T(8,128)S(1)} fusion(bf16[2,3072,768]{2,1,0:T(8,128)(2,1)} %param.26, f32[512,2,3072]{2,0,1:T(8,128)S(1)} %fusion.79), kind=kOutput, calls=%fused_computation.36 | convolution fusion | flops 4860149760 | bytes 25165824 | tf_op jit(solution)/shard_map/fte,fed->ftd/dot_general | solution.py:146
  85.0 6.1 fusion.34
  92.3 5.8 gather_fusion.2
  99.5 4.1 gather_fusion.3
  103.6 3.0 gather.27
  110.3 3.0 multiply_convert_fusion.5
  113.3 4.3 all-to-all-start.2
  117.5 2.3 reshape.485
  119.8 15.0 %fusion.26 = f32[816,3072]{1,0:T(8,128)S(1)} fusion(bf16[816,768]{1,0:T(8,128)(2,1)} %reshape.485, bf16[1,768,3072]{2,1,0:T(8,128)(2,1)} %param.27), kind=kOutput, calls=%fused_computation.45 | convolution fusion | flops 3850371072 | bytes 15998976 | tf_op jit(solution)/shard_map/erd,edf->erf/dot_general | solution.py:153
  134.9 11.8 %fusion.64 = bf16[1,816,768]{2,1,0:T(8,128)(2,1)S(1)} fusion(bf16[1,3072,768]{2,1,0:T(8,128)(2,1)} %param.28, f32[816,3072]{1,0:T(8,128)S(1)} %fusion.26), kind=kOutput, calls=%fused_computation.100 | convolution fusion | flops 3873558528 | bytes 15998976 | tf_op jit(solution)/shard_map/erf,efd->erd/dot_general | solution.py:155
  146.6 3.4 copy.116
  150.6 10.7 %reduce.10 = bf16[816,768]{1,0:T(8,128)(2,1)} reduce(bf16[816,1,768]{2,1,0:T(2,128)(2,1)} %bitcast.160, bf16[]{:T(256)} %broadcast.531), dimensions={1}, to_apply=%bitcast.148.reduce_sub_computation | reduce | bytes 2506754
  161.3 2.3 reshape.542
  163.5 4.3 all-to-all-start.1
  167.8 2.3 reshape.489
  170.1 12.1 %fusion.14 = bf16[816,3072]{1,0:T(8,128)(2,1)S(1)} fusion(f32[816,3072]{1,0:T(8,128)} %copy-done.68, bf16[816,768]{1,0:T(8,128)(2,1)} %reshape.489, bf16[1,3072,768]{2,1,0:T(8,128)(2,1)} %param.28), kind=kOutput, calls=%fused_computation.31 | convolution fusion | flops 3897999360 | bytes 21012480 | tf_op jit(solution)/shard_map/erd,efd->erf/dot_general | solution.py:193
  182.2 8.2 fusion.67
  190.4 3.4 copy.115
  193.8 10.5 %reduce.11 = bf16[816,768]{1,0:T(8,128)(2,1)} reduce(bf16[816,1,768]{2,1,0:T(2,128)(2,1)} %bitcast.161, bf16[]{:T(256)} %broadcast.531), dimensions={1}, to_apply=%bitcast.147.reduce_sub_computation | reduce | bytes 2506754
  204.3 2.3 reshape.544
  206.6 4.3 all-to-all-start.3
  214.4 3.4 multiply_reduce_fusion.1
  217.8 6.5 reshape.543
  224.3 2.9 copy.114
  228.5 6.5 reshape.545
  235.0 2.9 copy.113
  237.9 7.0 gather_fusion.1
  244.9 7.0 gather_fusion.4
  252.0 5.9 fusion.33
  261.4 3.4 fusion.93
  264.8 21.5 %multiply_reduce_fusion.2 = (f32[768]{0:T(1024)}, f32[512]{0:T(512)}, f32[512]{0:T(512)}, f32[512,768]{1,0:T(8,128)}) fusion(f32[512]{0:T(512)S(1)} %copy-done.42, f32[512,768]{1,0:T(8,128)} %copy-done.2, f32[512]{0:T(512)S(1)} %broadcast_multiply_fusion.4, f32[768]{0:T(1024)S(1)} %copy-done.38, f32[512,768]{1,0:T(8,128)} %fusion.93, ...), kind=kOutput, calls=%fused_computation.89 | convolution fusion | flops 9729341440 | bytes 40912896 | tf_op jit(solution)/shard_map/fte,fde->td/dot_general | solution.py:185
  287.7 4.7 multiply_add_fusion.2
  296.7 7.5 fusion.70
  304.2 9.5 %multiply_reduce_fusion = (f32[12,512]{1,0:T(8,128)S(1)}, f32[12,512,512]{1,2,0:T(8,128)}) fusion(f32[12,512]{1,0:T(8,128)S(1)} %copy-done.34, f32[12,512,512]{1,2,0:T(8,128)} %copy-done.1, pred[512,512]{0,1:T(8,128)(4,1)S(1)} %copy-done.13, bf16[512,12,64]{0,2,1:T(8,128)(2,1)S(1)} %bitcast.167, bf16[512,12,64]{0,2,1:T(8,128)(2,1)S(1)} %bitcast.165), kind=kOutput, calls=%fused_computation.18 | convolution fusion | flops 418375680 | bytes 27049984 | tf_op jit(solution)/shard_map/qhd,khd->hqk/dot_general | solution.py:225
  313.8 7.1 multiply_convert_fusion
  324.5 2.4 fusion.112
  327.0 2.4 fusion.114
  329.4 2.4 fusion.116
  333.2 11.2 %fusion.29 = bf16[1,3072,768]{2,1,0:T(8,128)(2,1)} fusion(bf16[816,768]{1,0:T(8,128)(2,1)S(1)} %copy-done.24, f32[816,3072]{1,0:T(8,128)} %copy-done.68), kind=kOutput, calls=%fused_computation.48 | convolution fusion | flops 3875291136 | bytes 15998976 | tf_op jit(solution)/shard_map/erf,erd->efd/dot_general | solution.py:206
  345.7 9.3 %fusion.28 = bf16[1,768,3072]{2,1,0:T(8,128)(2,1)} fusion(bf16[816,768]{1,0:T(8,128)(2,1)S(1)} %copy-done.23, bf16[816,3072]{1,0:T(8,128)(2,1)} %copy-done.66), kind=kOutput, calls=%fused_computation.47 | convolution fusion | flops 3852730368 | bytes 10985472 | tf_op jit(solution)/shard_map/erd,erf->edf/dot_general | solution.py:205
  355.1 116.9 %all-reduce.7.cloned.1.call-done = (f32[768,768]{1,0:T(8,128)}, f32[768,768]{1,0:T(8,128)}, f32[768,768]{1,0:T(8,128)}, f32[768,768]{1,0:T(8,128)}) async-done(((f32[768,768]{1,0:T(8,128)}, f32[768,768]{1,0:T(8,128)}, f32[768,768]{1,0:T(8,128)}, f32[768,768]{1,0:T(8,128)}), (f32[768,768]{1,0:T(8,128)}, f32[768,768]{1,0:T(8,128)}, f32[768,768]{1,0:T(8,128)}, ...) | async-done | bytes 9437200 | tf_op jit(solution)/shard_map/psum | solution.py:261
  473.4 2.7 fusion.74
  476.1 2.3 fusion.127
  479.6 3.1 fusion.53
  482.7 25.0 %all-reduce = (f32[768]{0:T(1024)}, f32[768]{0:T(1024)}, f32[768,10]{0,1:T(8,128)}) all-reduce(f32[768]{0:T(1024)S(1)} %get-tuple-element.13, f32[768]{0:T(1024)} %get-tuple-element.11, f32[768,10]{0,1:T(8,128)} %fusion.74), channel_id=1, replica_groups=mesh['dp'=4,'expert'=8] {'expert'}, use_global_device_ids=true, to_apply=%region_29.30 | all-reduce | flops 9216 | bytes 73728 | tf_op jit(solution)/shard_map/psum | solution.py:261
  507.7 21.6 %all-reduce.2 = (f32[768]{0:T(1024)}, f32[768]{0:T(1024)}, f32[768,10]{0,1:T(8,128)}) all-reduce(f32[768]{0:T(1024)} %get-tuple-element.25, f32[768]{0:T(1024)} %get-tuple-element.26, f32[768,10]{0,1:T(8,128)} %get-tuple-element.27), channel_id=1, replica_groups=mesh['dp'=4,'expert'=8] {'dp'}, use_global_device_ids=true, to_apply=%region_30.31 | all-reduce | flops 9216 | bytes 73728 | tf_op jit(solution)/shard_map/psum | solution.py:260
  530.7 3.1 fusion.52
  533.8 2.8 convert_element_type.180
  536.6 2.8 convert_element_type.177
  539.5 310.7 %all-reduce.9.cloned.1.call-done = (f32[768,768]{1,0:T(8,128)}, f32[768,768]{1,0:T(8,128)}, f32[768,768]{1,0:T(8,128)}, f32[768,768]{1,0:T(8,128)}) async-done(((f32[768,768]{1,0:T(8,128)}, f32[768,768]{1,0:T(8,128)}, f32[768,768]{1,0:T(8,128)}, f32[768,768]{1,0:T(8,128)}), (f32[768,768]{1,0:T(8,128)}, f32[768,768]{1,0:T(8,128)}, f32[768,768]{1,0:T(8,128)}, ...) | async-done | bytes 9437200 | tf_op jit(solution)/shard_map/psum | solution.py:260
  850.2 3.4 copy.126
  (226 shorter events, 54.4 us)
Async XLA Ops:
  8.0 17.3 %copy-start = (bf16[768,768]{1,0:T(8,128)(2,1)S(1)}, bf16[768,768]{1,0:T(8,128)(2,1)}, u32[]{:S(2)}) copy-start(bf16[768,768]{1,0:T(8,128)(2,1)} %param.21) | copy-start | bytes 3538948
  12.1 13.2 %copy-start.48 = (f32[512]{0:T(512)}, f32[512]{0:T(512)S(1)}, u32[]{:S(2)}) copy-start(f32[512]{0:T(512)S(1)} %broadcast_multiply_fusion.5) | copy-start | bytes 6148
  13.6 11.7 %copy-start.53 = (f32[512]{0:T(512)}, f32[512]{0:T(512)S(1)}, u32[]{:S(2)}) copy-start(f32[512]{0:T(512)S(1)} %add_rsqrt_fusion.1) | copy-start | bytes 6148
  14.4 31.7 %copy-start.44 = (s32[512,1]{0,1:T(1,128)}, s32[512,1]{0,1:T(1,128)S(1)}, u32[]{:S(2)}) copy-start(s32[512,1]{0,1:T(1,128)S(1)} %get-tuple-element.50) | copy-start | bytes 6148
  14.4 32.7 %copy-start.43 = (s32[512,1]{0,1:T(1,128)}, s32[512,1]{0,1:T(1,128)S(1)}, u32[]{:S(2)}) copy-start(s32[512,1]{0,1:T(1,128)S(1)} %get-tuple-element.49) | copy-start | bytes 6148
  17.9 2.7 copy-start.6
  20.6 9.5 %copy-start.8 = (bf16[512,768]{0,1:T(8,128)(2,1)}, bf16[512,768]{0,1:T(8,128)(2,1)S(1)}, u32[]{:S(2)}) copy-start(bf16[512,768]{0,1:T(8,128)(2,1)S(1)} %copy.82) | copy-start | bytes 2359300
  25.4 4.8 copy-start.10
  33.1 4.6 copy-start.1
  33.1 4.6 copy-start.33
  33.2 4.6 copy-start.12
  33.2 4.6 copy-start.14
  37.0 4.7 copy-start.36
  37.8 3.9 copy-start.63
  42.6 6.1 copy-start.2
  42.6 3.3 copy-start.39
  42.6 3.4 copy-start.37
  42.7 3.4 copy-start.62
  43.0 10.8 %copy-start.41 = (f32[512]{0:T(512)}, f32[512]{0:T(512)S(1)}, u32[]{:S(2)}) copy-start(f32[512]{0:T(512)S(1)} %add_rsqrt_fusion) | copy-start | bytes 6148
  44.7 3.6 copy-start.32
  46.0 2.3 copy-start.46
  46.0 2.3 copy-start.51
  46.0 2.3 copy-start.45
  47.1 1.9 copy-start.61
  49.1 7.0 copy-start.60
  49.8 4.1 copy-start.47
  58.6 54.6 %all-to-all-start = ((bf16[8,102,768]{2,1,0:T(8,128)(2,1)}), bf16[8,102,768]{2,1,0:T(8,128)(2,1)}, u32[]{:S(2)}, u32[]{:S(2)}) async-start(bf16[8,102,768]{2,1,0:T(8,128)(2,1)} %broadcast_select_fusion), calls=%async_computation | async-start | bytes 2555904 | tf_op jit(solution)/shard_map/all_to_all | solution.py:152
  71.4 13.5 %copy-start.67 = (f32[512,2,3072]{2,0,1:T(8,128)}, f32[512,2,3072]{2,0,1:T(8,128)S(1)}, u32[]{:S(2)}) copy-start(f32[512,2,3072]{2,0,1:T(8,128)S(1)} %fusion.79) | copy-start | bytes 37748740
  71.4 13.5 %copy-start.16 = (bf16[512,768]{1,0:T(8,128)(2,1)S(1)}, bf16[512,768]{1,0:T(8,128)(2,1)}, u32[]{:S(2)}) copy-start(bf16[512,768]{1,0:T(8,128)(2,1)} %param.29) | copy-start | bytes 2359300
  84.9 6.1 copy-start.17
  103.6 4.7 copy-start.40
  113.3 50.3 %all-to-all-start.2 = ((bf16[8,102,768]{2,1,0:T(8,128)(2,1)}), bf16[8,102,768]{2,1,0:T(8,128)(2,1)}, u32[]{:S(2)}, u32[]{:S(2)}) async-start(bf16[8,102,768]{2,1,0:T(8,128)(2,1)} %multiply_convert_fusion.5), calls=%async_computation.2 | async-start | bytes 2555904 | tf_op jit(solution)/shard_map/all_to_all | solution.py:192
  134.8 11.8 %copy-start.68 = (f32[816,3072]{1,0:T(8,128)}, f32[816,3072]{1,0:T(8,128)S(1)}, u32[]{:S(2)}) copy-start(f32[816,3072]{1,0:T(8,128)S(1)} %fusion.26) | copy-start | bytes 30081028
  163.5 43.0 %all-to-all-start.1 = ((bf16[8,2,39168]{2,1,0:T(2,128)(2,1)}), bf16[8,2,39168]{2,1,0:T(2,128)(2,1)}, u32[]{:S(2)}, u32[]{:S(2)}) async-start(bf16[8,2,39168]{2,1,0:T(2,128)(2,1)} %reshape.542), calls=%async_computation.1 | async-start | bytes 2506752 | tf_op jit(solution)/shard_map/all_to_all | solution.py:156
  182.2 8.2 copy-start.66
  206.6 21.9 %all-to-all-start.3 = ((bf16[8,2,39168]{2,1,0:T(2,128)(2,1)}), bf16[8,2,39168]{2,1,0:T(2,128)(2,1)}, u32[]{:S(2)}, u32[]{:S(2)}) async-start(bf16[8,2,39168]{2,1,0:T(2,128)(2,1)} %reshape.544), calls=%async_computation.3 | async-start | bytes 2506752 | tf_op jit(solution)/shard_map/all_to_all | solution.py:198
  210.8 261.2 %all-reduce.7.cloned.1.call-start = ((), (), s32[]{:S(2)}) async-start(), calls=%async_computation.8 | async-start | bytes 18874368 | tf_op jit(solution)/shard_map/psum | solution.py:261
  252.0 12.9 %copy-start.42 = (f32[512]{0:T(512)S(1)}, f32[512]{0:T(512)}, u32[]{:S(2)}) copy-start(f32[512]{0:T(512)} %copy-done.41) | copy-start | bytes 6148
  261.4 24.9 %copy-start.52 = (f32[512]{0:T(512)}, f32[512]{0:T(512)S(1)}, u32[]{:S(2)}) copy-start(f32[512]{0:T(512)S(1)} %multiply_reduce_fusion.7) | copy-start | bytes 6148
  287.7 4.7 copy-start.64
  292.5 1.7 copy-start.26
  294.1 2.5 copy-start.13
  294.2 2.5 copy-start.34
  296.7 7.6 copy-start.15
  296.7 17.1 %slice-start = ((s8[12582912]{0:T(1024)(128)(4,1)}), s8[4194304]{0:T(1024)(128)(4,1)S(1)}, s32[]{:S(2)}) async-start(s8[12582912]{0:T(1024)(128)(4,1)} %bitcast.152), calls=%async_computation.10 | async-start | bytes 8388608
  296.7 17.1 %slice-start.1 = ((s8[12582912]{0:T(1024)(128)(4,1)}), s8[4194304]{0:T(1024)(128)(4,1)S(1)}, s32[]{:S(2)}) async-start(s8[12582912]{0:T(1024)(128)(4,1)} %bitcast.152), calls=%async_computation.11 | async-start | bytes 8388608
  304.2 9.5 %slice-start.2 = ((s8[12582912]{0:T(1024)(128)(4,1)}), s8[4194304]{0:T(1024)(128)(4,1)S(1)}, s32[]{:S(2)}) async-start(s8[12582912]{0:T(1024)(128)(4,1)} %bitcast.152), calls=%async_computation.12 | async-start | bytes 8388608
  313.8 7.1 copy-start.11
  320.8 2.0 copy-start.9
  322.9 4.1 copy-start.29
  322.9 1.6 copy-start.27
  322.9 1.6 copy-start.49
  322.9 1.6 copy-start.54
  322.9 1.6 copy-start.57
  324.1 5.4 copy-start.18
  331.9 201.9 %reduce-scatter.5.cloned.1.call-start = ((), (), s32[]{:S(2)}) async-start(), calls=%async_computation.7 | async-start | bytes 5898240 | tf_op jit(solution)/shard_map/reduce_scatter | solution.py:211
  344.4 192.2 %reduce-scatter.3.cloned.1.call-start = ((), (), s32[]{:S(2)}) async-start(), calls=%async_computation.6 | async-start | bytes 5898240 | tf_op jit(solution)/shard_map/reduce_scatter | solution.py:208
  355.1 495.1 %all-reduce.9.cloned.1.call-start = ((), (), s32[]{:S(2)}) async-start(), calls=%async_computation.9 | async-start | bytes 18874368 | tf_op jit(solution)/shard_map/psum | solution.py:260
  473.4 5.1 copy-start.19
  473.4 5.1 copy-start.65
  479.6 51.1 %copy-start.5 = (f32[512,768]{1,0:T(8,128)S(1)}, f32[512,768]{1,0:T(8,128)}, u32[]{:S(2)}) copy-start(f32[512,768]{1,0:T(8,128)} %copy-done.4) | copy-start | bytes 4718596
  850.2 3.4 copy-start.22
  853.6 2.5 copy-start.21
  856.1 2.5 copy-start.20
  (16 other events, 17.2 us)
Sparse Core Ops, SparseCore 0:
  332.0 139.9 all-reduce.6
Sparse Core Ops, SparseCore 1:
  344.5 86.1 reduce-scatter.4
  432.9 86.7 reduce-scatter.2
  522.6 327.5 all-reduce.8
